TPU v7x, 128 devices: a whole 4x4x4 slice. The times are simulated.
128 devices in a mesh: grp: 16 (over y_lo, x, core), blk: 8 (over y_hi, z).
Axes of the slice: x: 4, y: 4 (y_hi: 2, y_lo: 2; y = y_hi * 2 + y_lo), z: 4, core: 2. Of those that a mesh axis runs over, the one named last changes fastest.
Arguments:
- pixels: bfloat16 [32, 262144], P(None, ('grp', 'blk')), may hold values from -6 to 6
- landmark_index: int32 [1, 16384], P(None, ('grp', 'blk')), may hold values from 0 to 2047
- counts: int32 [1, 128], P(None, ('grp', 'blk')), may hold values from 64 to 128, as said below
- factor: bfloat16 [64, 16384], P(None, ('grp', 'blk')), may hold values from -6 to 6
Outputs:
- embedding: float32 [64, 262144], P(None, ('grp', 'blk'))
- log_degree: float32 [1, 262144], P(None, ('grp', 'blk'))
Inputs may be any that keep to these rules, and one draw needn't show every extreme that they name: `landmark_index`: landmark slots of one device point at that device's own pixels. `counts`: some device has all 128 slots live in every draw.
All inputs are finite; a program needn't handle non-finite values.
Results may differ from a plain program's by a relative error of at most 0.0042.
Values may be sent and summed in bfloat16 or wider, within the bound.
No kernel may reach another device: no remote copies, remote signals or barrier semaphores. Data moves between devices by JAX's collectives and lax.ppermute only.
A program may use at most 64 MiB of HBM per device.

v0:
```python
import jax
import jax.numpy as jnp
from jax import lax
from jax.sharding import PartitionSpec as P

LAYERS = 32


def per_device(pixels, landmark_index, counts, factor):
    slot_cap = landmark_index.shape[1]
    pix_cols = pixels.shape[1]
    land = jnp.take(pixels, landmark_index[0], axis=1)
    pix_sq = jnp.sum(jnp.square(pixels.astype(jnp.float32)), axis=0, keepdims=True)

    def block_terms(land_blk, fac_blk, mask_blk):
        cross = lax.dot_general(
            land_blk, pixels, (((0,), (0,)), ((), ())), preferred_element_type=jnp.float32
        )
        land_sq = jnp.sum(jnp.square(land_blk.astype(jnp.float32)), axis=0)[:, None]
        dist = land_sq + pix_sq - 2.0 * cross
        kern = jnp.where(mask_blk, jnp.exp(-(2.0 / LAYERS) * dist), 0.0).astype(jnp.bfloat16)
        emb_add = jnp.dot(fac_blk, kern, preferred_element_type=jnp.float32)
        deg_add = jnp.sum(kern.astype(jnp.float32), axis=0, keepdims=True)
        return (emb_add, deg_add)

    emb_sum = jnp.zeros((factor.shape[0], pix_cols), jnp.float32)
    deg_sum = jnp.zeros((1, pix_cols), jnp.float32)
    land_part = lax.all_gather(land, ("grp", "blk"), axis=1, tiled=True)
    fac_part = lax.all_gather(factor, ("grp", "blk"), axis=1, tiled=True)
    cnt_part = lax.all_gather(counts, ("grp", "blk"), axis=1, tiled=True)
    columns = land_part.shape[1]
    live_mask = jnp.arange(slot_cap)[None, :] < cnt_part[0][:, None]
    live_mask = live_mask.reshape(columns, 1)
    live = jnp.sum(cnt_part.astype(jnp.float32))
    block = 256

    def turn(which, sums):
        land_blk = lax.dynamic_slice_in_dim(land_part, which * block, block, 1)
        fac_blk = lax.dynamic_slice_in_dim(fac_part, which * block, block, 1)
        mask_blk = lax.dynamic_slice_in_dim(live_mask, which * block, block, 0)
        emb_add, deg_add = block_terms(land_blk, fac_blk, mask_blk)
        return (sums[0] + emb_add, sums[1] + deg_add)

    emb_sum, deg_sum = lax.fori_loop(0, columns // block, turn, (emb_sum, deg_sum))
    raw_sum, degree, live = (emb_sum, deg_sum, live)
    scaled = raw_sum * lax.rsqrt(degree)
    squares = lax.psum(jnp.sum(scaled * scaled, axis=1, keepdims=True), ("grp", "blk"))
    total_pixels = pix_cols * lax.axis_size("grp") * lax.axis_size("blk")
    norms = jnp.sqrt(squares / total_pixels + 1e-06)
    return (scaled / norms, jnp.log(degree / live))


def solution(mesh):
    placed = (
        P(None, ("grp", "blk")),
        P(None, ("grp", "blk")),
        P(None, ("grp", "blk")),
        P(None, ("grp", "blk")),
    )
    return jax.shard_map(
        per_device,
        mesh=mesh,
        in_specs=placed,
        out_specs=(P(None, ("grp", "blk")), P(None, ("grp", "blk"))),
        check_vma=False,
    )
```

profile of v0, /device:TPU:1, one launch (start us, length us, event | category | flops | bytes accessed | tf_op | source)
XLA Modules:
  0.0 776.7 jit_solution(3649320138331622154)
XLA Ops:
  8.5 1.2 copy.6
  12.6 68.7 %all-reduce = s32[128]{0:T(128)S(1)} all-reduce(s32[128]{0:T(128)S(1)} %bitcast_dynamic-update-slice_fusion), channel_id=1, replica_groups=mesh['grp'=16,'blk'=8] {'grp','blk'}, use_global_device_ids=true, to_apply=%add | all-reduce | flops 128 | bytes 1024
  83.1 236.8 %all-gather.5.cloned.1.call-done = bf16[32,16384]{0,1:T(8,128)(2,1)} async-done(((bf16[32,128]{0,1:T(8,128)(2,1)}), bf16[32,16384]{0,1:T(8,128)(2,1)}) %all-gather.5.cloned.1.call-update) | async-done | bytes 1048592 | tf_op jit(solution)/shard_map/all_gather | solution.py:28
  319.9 3.5 copy.7
  323.4 251.1 %all-gather.3.cloned.1.call-done = bf16[64,16384]{1,0:T(8,128)(2,1)} async-done(((bf16[64,128]{1,0:T(8,128)(2,1)}), bf16[64,16384]{1,0:T(8,128)(2,1)}) %all-gather.3.cloned.1.call-update) | async-done | bytes 2097168 | tf_op jit(solution)/shard_map/all_gather | solution.py:29
  574.5 129.9 %while.16 = (s32[]{:T(128)}, f32[64,2048]{1,0:T(8,128)S(1)}, f32[1,2048]{1,0:T(1,128)S(1)}, bf16[64,16384]{1,0:T(8,128)(2,1)}, pred[16384,1]{0,1:T(4,128)(4,1)S(...) while((s32[]{:T(128)}, f32[64,2048]{1,0:T(8,128)S(1)}, ...), condition=%wide.region_4.5_spmd.clone, body=%wide.region_1.0_spmd.clone.sunk | while | flops 105146112 | bytes 3386558 | solution.py:44
  575.4 1.1 convolution_add_fusion.2
  577.4 1.1 convolution_add_fusion.2
  579.4 1.1 convolution_add_fusion.2
  581.4 1.1 convolution_add_fusion.2
  583.5 1.1 convolution_add_fusion.2
  585.5 1.1 convolution_add_fusion.2
  587.5 1.1 convolution_add_fusion.2
  589.6 1.1 convolution_add_fusion.2
  591.6 1.1 convolution_add_fusion.2
  593.6 1.1 convolution_add_fusion.2
  595.6 1.1 convolution_add_fusion.2
  597.7 1.1 convolution_add_fusion.2
  599.7 1.1 convolution_add_fusion.2
  601.7 1.1 convolution_add_fusion.2
  603.8 1.1 convolution_add_fusion.2
  605.8 1.1 convolution_add_fusion.2
  607.8 1.1 convolution_add_fusion.2
  609.9 1.1 convolution_add_fusion.2
  611.9 1.1 convolution_add_fusion.2
  613.9 1.1 convolution_add_fusion.2
  615.9 1.1 convolution_add_fusion.2
  618.0 1.1 convolution_add_fusion.2
  620.0 1.1 convolution_add_fusion.2
  622.0 1.1 convolution_add_fusion.2
  624.1 1.1 convolution_add_fusion.2
  626.1 1.1 convolution_add_fusion.2
  628.1 1.1 convolution_add_fusion.2
  630.1 1.1 convolution_add_fusion.2
  632.2 1.1 convolution_add_fusion.2
  634.2 1.1 convolution_add_fusion.2
  636.2 1.1 convolution_add_fusion.2
  638.3 1.1 convolution_add_fusion.2
  640.3 1.1 convolution_add_fusion.2
  642.3 1.1 convolution_add_fusion.2
  644.4 1.1 convolution_add_fusion.2
  646.4 1.1 convolution_add_fusion.2
  648.4 1.1 convolution_add_fusion.2
  650.4 1.1 convolution_add_fusion.2
  654.5 1.1 convolution_add_fusion.2
  695.1 1.1 convolution_add_fusion.2
  704.3 1.2 divide_log_fusion
  705.7 63.2 %psum.7 = f32[64,1]{0,1:T(1,128)S(1)} all-reduce(f32[64,1]{0,1:T(1,128)S(1)} %bitcast.40), channel_id=1, replica_groups=mesh['grp'=16,'blk'=8] {'grp','blk'}, use_global_device_ids=true, to_apply=%region_6.7 | all-reduce | flops 64 | bytes 512 | tf_op jit(solution)/shard_map/psum | solution.py:47
  (302 shorter events, 89.9 us)
Async XLA Ops:
  7.2 312.7 %all-gather.5.cloned.1.call-start = ((), (), s32[]{:S(2)}) async-start(), calls=%async_computation.1 | async-start | bytes 4227072 | tf_op jit(solution)/shard_map/all_gather | solution.py:28
  11.2 563.3 %all-gather.3.cloned.1.call-start = ((), (), s32[]{:S(2)}) async-start(), calls=%async_computation | async-start | bytes 2113536 | tf_op jit(solution)/shard_map/all_gather | solution.py:29
  83.1 491.4 %copy-start = (bf16[32,2048]{1,0:T(8,128)(2,1)S(1)}, bf16[32,2048]{1,0:T(8,128)(2,1)}, u32[]{:S(2)}) copy-start(bf16[32,2048]{1,0:T(8,128)(2,1)} %param.6) | copy-start | bytes 393220
Sparse Core Ops, SparseCore 0:
  11.3 308.5 all-gather.4
  321.5 252.8 all-gather.2
where the time goes:
time: 781 us; the launch traced here: 777 us
  waiting for transfers between devices  489 us (63%)
  blocking collectives  132 us (17%)
  matrix products  122 us (16%)
  between operations  14.8 us (2%)
  other arithmetic  9.17 us (1%)
    all_gather x1, waiting for transfers between devices, per_device(): fac_part = lax.all_gather(factor, ('grp', 'blk'), axis=1, tiled=True)  251 us
    all_gather x1, waiting for transfers between devices, per_device(): land_part = lax.all_gather(land, ('grp', 'blk'), axis=1, tiled=True)  237 us
    dot_general x64, matrix products, block_terms(): emb_add = jnp.dot(fac_blk, kern, preferred_element_type=jnp.float32)  69.7 us
    unnamed x1, blocking collectives  68.7 us
    psum x1, blocking collectives, per_device(): lax.psum(jnp.sum(scaled * scaled, axis=1, keepdims=True), ('grp', 'blk'))  63.2 us
    dot_general x64, matrix products, block_terms(): lax.dot_general(land_blk, pixels, (((0,), (0,)), ((), ())), preferred_ele...  52.6 us
  transfers between devices with their start and end apart: 2, of which 2 were waited for; matrix products, arithmetic and copies ran while one was open for 1% of the time, Pallas kernels for 0%

commit v1 on v0

v1 whole, which is shorter than its diff:
```python
import functools

import jax
import jax.numpy as jnp
import numpy as np
from jax import lax
from jax.experimental import pallas as pl
from jax.experimental.pallas import tpu as pltpu
from jax.sharding import Mesh
from jax.sharding import PartitionSpec as P

LAYERS = 32
EMB = 64
LIVE = EMB
LAND = 80
EXTRA = LAND + LAYERS
FEAT = 128
SCALE = float(np.log2(np.e) * 2.0 / LAYERS)
AXES = ("ylo", "x", "core", "yhi", "z")
CHIPS = ("ylo", "x", "yhi", "z")


def pieces(row):
    high = row.astype(jnp.bfloat16).astype(jnp.float32)
    middle = (row - high).astype(jnp.bfloat16).astype(jnp.float32)
    return high, middle, row - high - middle


def stack_rows(rows, count, width):
    at = lax.broadcasted_iota(jnp.int32, (count, width), 0)
    out = jnp.zeros((count, width), jnp.float32)
    for i, row in enumerate(rows):
        out = jnp.where(at == i, row, out)
    return out


def prepare_kernel(counts_ref, pixels_ref, index_ref, factor_ref, record_ref, pixop_ref):
    slots, width = index_ref.shape[1], pixels_ref.shape[1]
    pixels = pixels_ref[...]
    picked = lax.broadcasted_iota(jnp.int32, (width, slots), 0) == index_ref[...]
    land = jnp.dot(pixels, picked.astype(jnp.bfloat16), preferred_element_type=jnp.float32)
    land_sq = jnp.sum(land * land, axis=0, keepdims=True)
    live = lax.broadcasted_iota(jnp.int32, (1, slots), 1) < counts_ref[0, 0]
    factor = jnp.where(live, factor_ref[...].astype(jnp.float32), 0.0)
    ones = jnp.ones((1, slots), jnp.float32)
    record = jnp.concatenate(
        [
            factor,
            stack_rows([live.astype(jnp.float32)], LAND - EMB, slots),
            land,
            stack_rows([-p for p in pieces(land_sq)] + [ones] * 3, FEAT - EXTRA, slots),
        ],
        axis=0,
    )
    record_ref[...] = record.T.astype(jnp.bfloat16)
    wide = pixels.astype(jnp.float32)
    pix_sq = jnp.sum(wide * wide, axis=0, keepdims=True)
    ones = jnp.ones((1, width), jnp.float32)
    pixop_ref[:LAND, :] = jnp.zeros((LAND, width), jnp.bfloat16)
    pixop_ref[LAND:EXTRA, :] = (2.0 * wide).astype(jnp.bfloat16)
    pixop_ref[EXTRA:, :] = stack_rows(
        [ones] * 3 + [-p for p in pieces(pix_sq)], FEAT - EXTRA, width
    ).astype(jnp.bfloat16)


def prepare(pixels, landmark_index, counts, factor):
    slots, width = landmark_index.shape[1], pixels.shape[1]
    vmem = pl.BlockSpec(memory_space=pltpu.VMEM)
    return pl.pallas_call(
        prepare_kernel,
        out_shape=(
            jax.ShapeDtypeStruct((slots, FEAT), jnp.bfloat16),
            jax.ShapeDtypeStruct((FEAT, width), jnp.bfloat16),
        ),
        in_specs=[pl.BlockSpec(memory_space=pltpu.SMEM), vmem, vmem, vmem],
        out_specs=(vmem, vmem),
        name="prepare",
    )(counts, pixels, landmark_index, factor)


def accumulate_kernel(first, tile, record_ref, pixop_ref, *refs):
    sums_ref = refs[-1]
    if first:
        sums_ref[...] = jnp.zeros_like(sums_ref)
    else:
        sums_ref[...] = refs[0][...]

    def step(t, carry):
        record = record_ref[pl.ds(pl.multiple_of(t * tile, tile), tile), :]
        dist = jnp.dot(record, pixop_ref[...], preferred_element_type=jnp.float32)
        kern = jnp.exp2(dist * SCALE).astype(jnp.bfloat16)
        sums_ref[...] += jnp.dot(record.T[:LAND, :], kern, preferred_element_type=jnp.float32)
        return carry

    lax.fori_loop(0, record_ref.shape[0] // tile, step, 0)


def accumulate(records, pixop, sums=None, tile=1024):
    slots, width = records.shape[0], pixop.shape[1]
    vmem = pl.BlockSpec(memory_space=pltpu.VMEM)
    args = (records, pixop) + (() if sums is None else (sums,))
    return pl.pallas_call(
        functools.partial(accumulate_kernel, sums is None, tile),
        out_shape=jax.ShapeDtypeStruct((LAND, width), jnp.float32),
        in_specs=[vmem] * len(args),
        out_specs=vmem,
        input_output_aliases={} if sums is None else {2: 0},
        cost_estimate=pl.CostEstimate(
            flops=2 * slots * width * 256,
            bytes_accessed=2 * slots * FEAT,
            transcendentals=slots * width,
        ),
        compiler_params=pltpu.CompilerParams(vmem_limit_bytes=48 << 20),
        name="accumulate",
    )(*args)


def scale_kernel(counts_ref, sums_ref, scaled_ref, total_ref):
    scaled = sums_ref[:EMB, :] * lax.rsqrt(sums_ref[LIVE : LIVE + 1, :])
    scaled_ref[...] = scaled
    squares = jnp.sum(scaled * scaled, axis=1, keepdims=True)
    row = jnp.broadcast_to(squares, (EMB, FEAT)).T[:1, :]
    live = jnp.full((1, FEAT - EMB), counts_ref[0, 0].astype(jnp.float32))
    total_ref[...] = jnp.concatenate([row, live], axis=1)


def scale(counts, sums):
    vmem = pl.BlockSpec(memory_space=pltpu.VMEM)
    return pl.pallas_call(
        scale_kernel,
        out_shape=(
            jax.ShapeDtypeStruct((EMB, sums.shape[1]), jnp.float32),
            jax.ShapeDtypeStruct((1, FEAT), jnp.float32),
        ),
        in_specs=[pl.BlockSpec(memory_space=pltpu.SMEM), vmem],
        out_specs=(vmem, vmem),
        name="scale",
    )(counts, sums)


def finish_kernel(pixel_count, totals_ref, scaled_ref, sums_ref, embedding_ref, log_ref):
    total = jnp.sum(totals_ref[...], axis=0, keepdims=True)
    live = jnp.sum(total[:, LIVE : LIVE + 1])
    norms = jnp.sqrt(jnp.broadcast_to(total, (FEAT, FEAT)).T[:EMB, :1] / pixel_count + 1e-06)
    embedding_ref[...] = scaled_ref[...] * (1.0 / norms)
    log_ref[...] = jnp.log(sums_ref[LIVE : LIVE + 1, :] / live)


def finish(totals, scaled, sums):
    width = scaled.shape[1]
    vmem = pl.BlockSpec(memory_space=pltpu.VMEM)
    return pl.pallas_call(
        functools.partial(finish_kernel, float(width * totals.shape[0])),
        out_shape=(
            jax.ShapeDtypeStruct((EMB, width), jnp.float32),
            jax.ShapeDtypeStruct((1, width), jnp.float32),
        ),
        in_specs=[vmem] * 3,
        out_specs=(vmem, vmem),
        name="finish",
    )(totals, scaled, sums)


def to_all(x, axes):
    copies = jnp.broadcast_to(x[None], (lax.axis_size(axes),) + x.shape)
    return lax.all_to_all(copies, axes, 0, 0, tiled=True)


def per_device(pixels, landmark_index, counts, factor):
    record, pixop = prepare(pixels, landmark_index, counts, factor)
    records = to_all(record, CHIPS).reshape(-1, FEAT)
    others = lax.ppermute(records, "core", [(0, 1), (1, 0)])
    sums = accumulate(records, pixop)
    sums = accumulate(others, pixop, sums)
    scaled, total = scale(counts, sums)
    totals = to_all(total[0], AXES)
    return finish(totals, scaled, sums)


def solution(mesh):
    fine = Mesh(mesh.devices.reshape(2, 4, 2, 2, 4), AXES)
    placed = P(None, AXES)
    return jax.shard_map(
        per_device,
        mesh=fine,
        in_specs=(placed,) * 4,
        out_specs=(placed, placed),
        check_vma=False,
    )
```

time: 781 us -> 99.3 us (0.13)
  waiting for transfers between devices: 489 us -> 0.01 us
  matrix products: 122 us -> 0 us
  blocking collectives: 132 us -> 54 us
  Pallas kernels: 0 us -> 37.5 us
  between operations: 14.8 us -> 1.32 us
  other arithmetic: 9.17 us -> 0 us
    all_gather x2 -> x0, waiting for transfers between devices: 488 us -> none  [the longest x1 251 us: per_device(): fac_part = lax.all_gather(factor, ('grp', 'blk'), axis=1, tiled=True)]
    dot_general x128 -> x0, matrix products: 122 us -> none  [the longest x64 69.7 us: block_terms(): emb_add = jnp.dot(fac_blk, kern, preferred_element_type=jnp.float32)]
    unnamed x1 -> x0, blocking collectives: 68.7 us -> none
    psum x1 -> x0, blocking collectives: 63.2 us -> none  [per_device(): lax.psum(jnp.sum(scaled * scaled, axis=1, keepdims=True), ('grp', 'blk'))]
    all_to_all x0 -> x2, blocking collectives: none -> 54 us  [to_all(): return lax.all_to_all(copies, axes, 0, 0, tiled=True)]
    pallas_call x0 -> x5, Pallas kernels: none -> 37.5 us  [the longest x2 31.2 us: accumulate(): pl.pallas_call(functools.partial(accumulate_kernel, sums is None, tile),...]
  transfers between devices with their start and end apart: 2 -> 1, of which waited for: 2 -> 0; matrix products, arithmetic and copies ran while one was open for 1% -> 0% of each run, Pallas kernels for 0% -> 16%
where the time goes in v1:
time: 99.3 us; the launch traced here: 99 us
  blocking collectives  54 us (54%)
  Pallas kernels  37.5 us (38%)
  starting transfers between devices  3.35 us (3%)
  local copies, waits for them, and re-layouts  2.79 us (3%)
  between operations  1.32 us (1%)
    all_to_all x2, blocking collectives, to_all(): return lax.all_to_all(copies, axes, 0, 0, tiled=True)  54 us
    pallas_call x2, Pallas kernels, accumulate(): pl.pallas_call(functools.partial(accumulate_kernel, sums is None, tile),...  31.2 us
    ppermute x1, starting transfers between devices, per_device(): others = lax.ppermute(records, 'core', [(0, 1), (1, 0)])  3.35 us
    pallas_call x1, Pallas kernels, finish(): pl.pallas_call(functools.partial(finish_kernel, float(width * totals.shap...  2.28 us
    pallas_call x1, Pallas kernels, prepare(): pl.pallas_call(prepare_kernel, out_shape=(jax.ShapeDtypeStruct((slots, FE...  1.99 us
  transfers between devices with their start and end apart: 1, of which 0 were waited for; matrix products, arithmetic and copies ran while one was open for 0% of the time, Pallas kernels for 16%

profile of v1, /device:TPU:1, one launch (start us, length us, event | category | flops | bytes accessed | tf_op | source)
XLA Modules:
  0.0 99.0 jit_solution(3817264649940685683)
XLA Ops:
  1.3 2.0 %prepare.1 = (bf16[128,128]{1,0:T(8,128)(2,1)}, bf16[128,2048]{1,0:T(8,128)(2,1)}) custom-call(s32[1,1]{1,0:T(1,128)S(6)} %copy.8.counts_ref, bf16[32,2048]{1,0:T(8,128)(2,1)} %pixels_ref.1, s32[1,128]{1,0:T(1,128)} %index_ref.1, bf16[64,128]{1,0:T(8,128)(2,1)} %factor_ref.1), custom_call_target="tpu_custom_call" | custom-call | tf_op jit(solution)/shard_map/prepare/pallas_call | solution.py:69
  3.3 1.2 %broadcast_in_dim.4 = bf16[64,128,128]{2,1,0:T(8,128)(2,1)S(1)} broadcast(bf16[128,128]{1,0:T(8,128)(2,1)} %get-tuple-element.6), dimensions={1,2} | broadcast | bytes 2129920 | tf_op jit(solution)/shard_map/broadcast_in_dim | solution.py:165
  4.5 0.0 copy-start.1
  4.5 38.2 %all_to_all.13 = bf16[64,128,128]{2,1,0:T(8,128)(2,1)S(1)} all-to-all(bf16[64,128,128]{2,1,0:T(8,128)(2,1)S(1)} %broadcast_in_dim.4), channel_id=1, replica_groups=mesh['ylo'=2,'x'=4,'core'=2,'yhi'=2,'z'=4] {'ylo','x','yhi','z'}, dimensions={0} | all-to-all | bytes 4194304 | tf_op jit(solution)/shard_map/all_to_all | solution.py:166
  42.8 3.4 %collective-permute-start = (bf16[8192,128]{1,0:T(8,128)(2,1)S(1)}, bf16[8192,128]{1,0:T(8,128)(2,1)S(1)}, u32[]{:S(2)}, u32[]{:S(2)}) collective-permute-start(bf16[8192,128]{1,0:T(8,128)(2,1)S(1)} %bitcast.3), channel_id=1, source_target_pairs={{0,8},{8,0},{1,9},{9,1},{2,10},{10,2},{3,11},{11,3},{4,12},{12,4},... | collective-permute-start | bytes 6291464 | tf_op jit(solution)/shard_map/ppermute | solution.py:172
  46.1 0.0 copy-done.1
  46.1 15.6 %accumulate.2.refs_0_ = f32[80,2048]{1,0:T(8,128)S(1)} custom-call(bf16[8192,128]{1,0:T(8,128)(2,1)S(1)} %bitcast.4, bf16[128,2048]{1,0:T(8,128)(2,1)S(1)} %copy-done.1), custom_call_target="tpu_custom_call" | custom-call | flops 8589934592 | bytes 2097152 | tf_op jit(solution)/shard_map/accumulate/pallas_call | solution.py:102
  61.7 0.0 collective-permute-done.record_ref
  61.7 15.6 %accumulate.3.sums_ref = f32[80,2048]{1,0:T(8,128)S(1)} custom-call(bf16[8192,128]{1,0:T(8,128)(2,1)S(1)} %collective-permute-done.record_ref, bf16[128,2048]{1,0:T(8,128)(2,1)S(1)} %copy-done.1, f32[80,2048]{1,0:T(8,128)S(1)} %accumulate.2.refs_0_), custom_call_target="tpu_custom_call", output_to_operand_aliasing={{}: (2, {})} | custom-call | flops 8589934592 | bytes 2097152 | tf_op jit(solution)/shard_map/accumulate/pallas_call | solution.py:102
  77.4 0.0 copy-start
  77.4 0.8 copy-done
  78.2 1.9 %scale.1 = (f32[64,2048]{1,0:T(8,128)}, f32[1,128]{1,0:T(1,128)}) custom-call(s32[1,1]{1,0:T(1,128)S(6)} %copy.8.counts_ref, f32[80,2048]{1,0:T(8,128)} %copy-done), custom_call_target="tpu_custom_call" | custom-call | tf_op jit(solution)/shard_map/scale/pallas_call | solution.py:129
  80.2 0.7 broadcast_in_dim.5
  80.9 15.8 %all_to_all.14 = f32[128,1,128]{2,1,0:T(1,128)} all-to-all(f32[128,1,128]{2,1,0:T(1,128)S(1)} %broadcast_in_dim.5), channel_id=1, replica_groups=mesh['ylo'=2,'x'=4,'core'=2,'yhi'=2,'z'=4] {'ylo','x','core','yhi','z'}, dimensions={0} | all-to-all | bytes 131072 | tf_op jit(solution)/shard_map/all_to_all | solution.py:166
  96.7 2.3 %finish.1 = (f32[64,2048]{1,0:T(8,128)}, f32[1,2048]{1,0:T(1,128)}) custom-call(f32[128,128]{1,0:T(8,128)} %bitcast.5, f32[64,2048]{1,0:T(8,128)} %get-tuple-element.9.scaled_ref, f32[80,2048]{1,0:T(8,128)} %copy-done), custom_call_target="tpu_custom_call" | custom-call | tf_op jit(solution)/shard_map/finish/pallas_call | solution.py:152
Async XLA Ops:
  4.5 41.6 %copy-start.1 = (bf16[128,2048]{1,0:T(8,128)(2,1)S(1)}, bf16[128,2048]{1,0:T(8,128)(2,1)}, u32[]{:S(2)}) copy-start(bf16[128,2048]{1,0:T(8,128)(2,1)} %get-tuple-element.7.pixop_ref) | copy-start | bytes 1572868
  42.8 19.0 %collective-permute-start = (bf16[8192,128]{1,0:T(8,128)(2,1)S(1)}, bf16[8192,128]{1,0:T(8,128)(2,1)S(1)}, u32[]{:S(2)}, u32[]{:S(2)}) collective-permute-start(bf16[8192,128]{1,0:T(8,128)(2,1)S(1)} %bitcast.3), channel_id=1, source_target_pairs={{0,8},{8,0},{1,9},{9,1},{2,10},{10,2},{3,11},{11,3},{4,12},{12,4},... | collective-permute-start | bytes 6291464 | tf_op jit(solution)/shard_map/ppermute | solution.py:172
  77.4 0.9 copy-start

commit v2 on v1

v2 whole, which is shorter than its diff:
```python
import functools

import jax
import jax.numpy as jnp
import numpy as np
from jax import lax
from jax.experimental import pallas as pl
from jax.experimental.pallas import tpu as pltpu
from jax.sharding import Mesh
from jax.sharding import PartitionSpec as P

LAYERS = 32
EMB = 64
LIVE = EMB
LAND = 80
EXTRA = LAND + LAYERS
FEAT = 128
SCALE = float(np.log2(np.e) * 2.0 / LAYERS)
AXES = ("ylo", "x", "core", "yhi", "z")
SIZES = (2, 4, 2, 2, 4)
CAP = 128
COUNT = EXTRA + 6
GRAIN = 16
BIG = 1024
SMALL = 256


def pieces(row):
    high = row.astype(jnp.bfloat16).astype(jnp.float32)
    middle = (row - high).astype(jnp.bfloat16).astype(jnp.float32)
    return high, middle, row - high - middle


def stack_rows(rows, count, width):
    at = lax.broadcasted_iota(jnp.int32, (count, width), 0)
    out = jnp.zeros((count, width), jnp.float32)
    for i, row in enumerate(rows):
        out = jnp.where(at == i, row, out)
    return out


def record_kernel(counts_ref, pixels_ref, index_ref, factor_ref, record_ref):
    slots, width = index_ref.shape[1], pixels_ref.shape[1]
    picked = lax.broadcasted_iota(jnp.int32, (width, slots), 0) == index_ref[...]
    land = jnp.dot(
        pixels_ref[...], picked.astype(jnp.bfloat16), preferred_element_type=jnp.float32
    )
    land_sq = jnp.sum(land * land, axis=0, keepdims=True)
    live = lax.broadcasted_iota(jnp.int32, (1, slots), 1) < counts_ref[0, 0]
    factor = jnp.where(live, factor_ref[...].astype(jnp.float32), 0.0)
    ones = jnp.ones((1, slots), jnp.float32)
    count = ones * counts_ref[0, 0].astype(jnp.float32)
    record = jnp.concatenate(
        [
            factor,
            stack_rows([live.astype(jnp.float32)], LAND - EMB, slots),
            land,
            stack_rows([-p for p in pieces(land_sq)] + [ones] * 3 + [count], FEAT - EXTRA, slots),
        ],
        axis=0,
    )
    record_ref[...] = record.T.astype(jnp.bfloat16)


def make_record(pixels, landmark_index, counts, factor):
    vmem = pl.BlockSpec(memory_space=pltpu.VMEM)
    return pl.pallas_call(
        record_kernel,
        out_shape=jax.ShapeDtypeStruct((landmark_index.shape[1], FEAT), jnp.bfloat16),
        in_specs=[pl.BlockSpec(memory_space=pltpu.SMEM), vmem, vmem, vmem],
        out_specs=vmem,
        compiler_params=pltpu.CompilerParams(vmem_limit_bytes=16 << 20),
        name="record",
    )(counts, pixels, landmark_index, factor)


def operand_kernel(pixels_ref, pixop_ref):
    width = pixels_ref.shape[1]
    wide = pixels_ref[...].astype(jnp.float32)
    pix_sq = jnp.sum(wide * wide, axis=0, keepdims=True)
    ones = jnp.ones((1, width), jnp.float32)
    pixop_ref[:LAND, :] = jnp.zeros((LAND, width), jnp.bfloat16)
    pixop_ref[LAND:EXTRA, :] = (2.0 * wide).astype(jnp.bfloat16)
    pixop_ref[EXTRA:, :] = stack_rows(
        [ones] * 3 + [-p for p in pieces(pix_sq)], FEAT - EXTRA, width
    ).astype(jnp.bfloat16)


def make_operand(pixels):
    vmem = pl.BlockSpec(memory_space=pltpu.VMEM)
    return pl.pallas_call(
        operand_kernel,
        out_shape=jax.ShapeDtypeStruct((FEAT, pixels.shape[1]), jnp.bfloat16),
        in_specs=[vmem],
        out_specs=vmem,
        cost_estimate=pl.CostEstimate(
            flops=pixels.size * 8, bytes_accessed=pixels.size * 10, transcendentals=0
        ),
        compiler_params=pltpu.CompilerParams(vmem_limit_bytes=16 << 20),
        name="operand",
    )(pixels)


def accumulate_kernel(n_records, n_sides, first, *refs):
    record_refs, refs = refs[:n_records], refs[n_records:]
    pixop_refs, refs = refs[:n_sides], refs[n_sides:]
    packed_ref = refs[-1]
    sums_refs = refs[-1 - n_sides : -1]
    for i, sums_ref in enumerate(sums_refs):
        sums_ref[...] = jnp.zeros_like(sums_ref) if first else refs[i][...]

    rows = lax.broadcasted_iota(jnp.int32, (GRAIN, FEAT), 0)
    lanes = lax.broadcasted_iota(jnp.int32, (GRAIN, FEAT), 1)
    at_count = (rows == 0) & (lanes == COUNT)
    filled = jnp.int32(0)
    for record_ref in record_refs:
        for start in range(0, record_ref.shape[0], CAP):
            head = record_ref[start : start + GRAIN, :].astype(jnp.float32)
            count = jnp.sum(jnp.where(at_count, head, 0.0)).astype(jnp.int32)
            packed_ref[pl.ds(pl.multiple_of(filled, GRAIN), CAP), :] = record_ref[
                start : start + CAP, :
            ]
            filled += (count + (GRAIN - 1)) // GRAIN * GRAIN
    packed_ref[pl.ds(pl.multiple_of(filled, GRAIN), SMALL), :] = jnp.zeros(
        (SMALL, FEAT), jnp.bfloat16
    )

    def add(start, size):
        record = packed_ref[pl.ds(pl.multiple_of(start, SMALL), size), :]
        columns = record.T[:LAND, :]
        for pixop_ref, sums_ref in zip(pixop_refs, sums_refs, strict=True):
            dist = jnp.dot(record, pixop_ref[...], preferred_element_type=jnp.float32)
            kern = jnp.exp2(dist * SCALE).astype(jnp.bfloat16)
            sums_ref[...] += jnp.dot(columns, kern, preferred_element_type=jnp.float32)

    big = filled // BIG
    small = (filled - big * BIG + (SMALL - 1)) // SMALL
    lax.fori_loop(0, big, lambda t, c: (add(t * BIG, BIG), c)[1], 0)
    lax.fori_loop(0, small, lambda t, c: (add(big * BIG + t * SMALL, SMALL), c)[1], 0)


def accumulate(records, pixops, sums=()):
    slots, width, sides = sum(r.shape[0] for r in records), pixops[0].shape[1], len(pixops)
    vmem = pl.BlockSpec(memory_space=pltpu.VMEM)
    args = (*records, *pixops, *sums)
    return pl.pallas_call(
        functools.partial(accumulate_kernel, len(records), sides, not sums),
        out_shape=(jax.ShapeDtypeStruct((LAND, width), jnp.float32),) * sides,
        in_specs=[vmem] * len(args),
        out_specs=(vmem,) * sides,
        scratch_shapes=[pltpu.VMEM((slots + BIG, FEAT), jnp.bfloat16)],
        input_output_aliases={len(records) + sides + i: i for i in range(len(sums))},
        cost_estimate=pl.CostEstimate(
            flops=2 * slots * width * sides * 256,
            bytes_accessed=2 * slots * FEAT,
            transcendentals=slots * width * sides,
        ),
        compiler_params=pltpu.CompilerParams(vmem_limit_bytes=48 << 20),
        name="accumulate",
    )(*args)


def scale_kernel(counts_ref, mine_ref, theirs_ref, scaled_ref, degree_ref, total_ref):
    degree = mine_ref[LIVE : LIVE + 1, :] + theirs_ref[LIVE : LIVE + 1, :]
    degree_ref[...] = degree
    scaled = (mine_ref[:EMB, :] + theirs_ref[:EMB, :]) * lax.rsqrt(degree)
    scaled_ref[...] = scaled
    squares = jnp.sum(scaled * scaled, axis=1, keepdims=True)
    row = jnp.broadcast_to(squares, (EMB, FEAT)).T[:1, :]
    live = jnp.full((1, FEAT - EMB), counts_ref[0, 0].astype(jnp.float32))
    total_ref[...] = jnp.concatenate([row, live], axis=1)


def scale(counts, mine, theirs):
    width = mine.shape[1]
    vmem = pl.BlockSpec(memory_space=pltpu.VMEM)
    return pl.pallas_call(
        scale_kernel,
        out_shape=(
            jax.ShapeDtypeStruct((EMB, width), jnp.float32),
            jax.ShapeDtypeStruct((1, width), jnp.float32),
            jax.ShapeDtypeStruct((1, FEAT), jnp.float32),
        ),
        in_specs=[pl.BlockSpec(memory_space=pltpu.SMEM), vmem, vmem],
        out_specs=(vmem, vmem, vmem),
        compiler_params=pltpu.CompilerParams(vmem_limit_bytes=16 << 20),
        name="scale",
    )(counts, mine, theirs)


def finish_kernel(pixel_count, totals_ref, scaled_ref, degree_ref, embedding_ref, log_ref):
    total = jnp.sum(totals_ref[...], axis=0, keepdims=True)
    live = jnp.sum(total[:, LIVE : LIVE + 1])
    norms = jnp.sqrt(jnp.broadcast_to(total, (FEAT, FEAT)).T[:EMB, :1] / pixel_count + 1e-06)
    embedding_ref[...] = scaled_ref[...] * (1.0 / norms)
    log_ref[...] = jnp.log(degree_ref[...] / live)


def finish(totals, scaled, degree):
    width = scaled.shape[1]
    vmem = pl.BlockSpec(memory_space=pltpu.VMEM)
    return pl.pallas_call(
        functools.partial(finish_kernel, float(width * totals.shape[0])),
        out_shape=(
            jax.ShapeDtypeStruct((EMB, width), jnp.float32),
            jax.ShapeDtypeStruct((1, width), jnp.float32),
        ),
        in_specs=[vmem] * 3,
        out_specs=(vmem, vmem),
        compiler_params=pltpu.CompilerParams(vmem_limit_bytes=16 << 20),
        name="finish",
    )(totals, scaled, degree)


def to_all(x, axes):
    copies = jnp.broadcast_to(x[None], (lax.axis_size(axes),) + x.shape)
    return lax.all_to_all(copies, axes, 0, 0, tiled=True)


def moved(move):
    pairs = []
    for i in range(int(np.prod(SIZES))):
        ylo, x, core, yhi, z = (int(v) for v in np.unravel_index(i, SIZES))
        to = move({"x": x, "y": 2 * yhi + ylo, "z": z, "core": core})
        place = (to["y"] % 2, to["x"], to["core"], to["y"] // 2, to["z"])
        pairs.append((i, int(np.ravel_multi_index(place, SIZES))))
    return pairs


def along(axes, hops):
    def move(at):
        axis = axes[at["core"]]
        return {**at, axis: (at[axis] + hops) % 4}

    return moved(move)


def per_device(pixels, landmark_index, counts, factor):
    swap = moved(lambda at: {**at, "core": 1 - at["core"]})
    record = make_record(pixels, landmark_index, counts, factor)
    pixops = [make_operand(pixels), make_operand(lax.ppermute(pixels, AXES, swap))]
    gathered = record
    for axes in (("x", "y"), ("y", "z")):
        far, up, down = (lax.ppermute(gathered, AXES, along(axes, h)) for h in (2, 1, 3))
        gathered = jnp.concatenate([gathered, up, down, far], axis=0)
    last = ("z", "x")
    up = lax.ppermute(gathered, AXES, along(last, 1))
    down = lax.ppermute(gathered, AXES, along(last, 3))
    sums = accumulate([gathered], pixops)
    gathered, up, down = lax.optimization_barrier((gathered, up, down))
    far = lax.ppermute(gathered, AXES, along(last, 2))
    mine, theirs = accumulate([up, down], pixops, sums)
    (theirs,) = accumulate([far], pixops[1:], (theirs,))
    swapped = lax.ppermute(theirs, AXES, swap)
    (mine,) = accumulate([far], pixops[:1], (mine,))
    scaled, degree, total = scale(counts, mine, swapped)
    totals = to_all(total[0], AXES)
    return finish(totals, scaled, degree)


def solution(mesh):
    fine = Mesh(mesh.devices.reshape(SIZES), AXES)
    placed = P(None, AXES)
    return jax.shard_map(
        per_device,
        mesh=fine,
        in_specs=(placed,) * 4,
        out_specs=(placed, placed),
        check_vma=False,
    )
```

time: 99.3 us -> 76 us (0.77)
  blocking collectives: 54 us -> 13.7 us
  starting transfers between devices: 3.35 us -> 20.5 us
  waiting for transfers between devices: 0.01 us -> 8.07 us
  Pallas kernels: 37.5 us -> 29.9 us
  local copies, waits for them, and re-layouts: 2.79 us -> 1.76 us
    all_to_all x2 -> x1, blocking collectives: 54 us -> 13.7 us  [to_all(): return lax.all_to_all(copies, axes, 0, 0, tiled=True)]
    ppermute x1 -> x11, starting transfers between devices: 3.35 us -> 20.5 us  [the longest x6 10.4 us: per_device(): lax.ppermute(gathered, AXES, along(axes, h))]
    ppermute x1 -> x11, waiting for transfers between devices: 0.01 us -> 8.07 us  [the longest x6 5.9 us: per_device(): lax.ppermute(gathered, AXES, along(axes, h))]
    pallas_call x4 -> x8, Pallas kernels: 35.2 us -> 28.9 us  [the longest x4 28.2 us: accumulate(): pl.pallas_call(functools.partial(accumulate_kernel, len(records), sides,...]
    broadcast_in_dim x2 -> x1, local copies, waits for them, and re-layouts: 1.94 us -> 0.05 us  [to_all(): copies = jnp.broadcast_to(x[None], (lax.axis_size(axes),) + x.shape)]
    pallas_call x1, Pallas kernels: 2.28 us -> 1.01 us  [finish(): pl.pallas_call(functools.partial(finish_kernel, float(width * totals.shap...]
  transfers between devices with their start and end apart: 1 -> 11, of which waited for: 0 -> 3; matrix products, arithmetic and copies ran while one was open for 0% -> 0% of each run, Pallas kernels for 16% -> 32%
where the time goes in v2:
time: 76 us; the launch traced here: 75.3 us
  Pallas kernels  29.9 us (39%)
  starting transfers between devices  20.5 us (27%)
  blocking collectives  13.7 us (18%)
  waiting for transfers between devices  8.07 us (11%)
  local copies, waits for them, and re-layouts  1.76 us (2%)
  between operations  1.42 us (2%)
    pallas_call x4, Pallas kernels, accumulate(): pl.pallas_call(functools.partial(accumulate_kernel, len(records), sides,...  28.2 us
    all_to_all x1, blocking collectives, to_all(): return lax.all_to_all(copies, axes, 0, 0, tiled=True)  13.7 us
    ppermute x6, starting transfers between devices, per_device(): lax.ppermute(gathered, AXES, along(axes, h))  10.4 us
    ppermute x6, waiting for transfers between devices, per_device(): lax.ppermute(gathered, AXES, along(axes, h))  5.9 us
    ppermute x1, starting transfers between devices, per_device(): swapped = lax.ppermute(theirs, AXES, swap)  5.88 us
    ppermute x1, starting transfers between devices, per_device(): down = lax.ppermute(gathered, AXES, along(last, 3))  2.84 us
    ppermute x1, waiting for transfers between devices, per_device(): up = lax.ppermute(gathered, AXES, along(last, 1))  2.16 us
    unnamed x12, local copies, waits for them, and re-layouts  1.69 us
  transfers between devices with their start and end apart: 11, of which 3 were waited for; matrix products, arithmetic and copies ran while one was open for 0% of the time, Pallas kernels for 32%

profile of v2, /device:TPU:1, one launch (start us, length us, event | category | flops | bytes accessed | tf_op | source)
XLA Modules:
  0.0 75.3 jit_solution(12645086802535125159)
XLA Ops:
  0.6 0.0 copy-start.2
  1.3 0.0 copy-done.2
  1.3 0.0 copy-start
  1.3 0.9 %copy-done = bf16[32,2048]{1,0:T(8,128)(2,1)S(1)} copy-done((bf16[32,2048]{1,0:T(8,128)(2,1)S(1)}, bf16[32,2048]{1,0:T(8,128)(2,1)}, u32[]{:S(2)}) %copy-start) | copy-done | bytes 131096
  2.2 0.0 copy-start.1
  2.2 0.7 copy-done.1
  2.9 0.3 record.1
  3.2 3.8 %collective-permute-start.2 = (bf16[128,128]{1,0:T(8,128)(2,1)S(1)}, bf16[128,128]{1,0:T(8,128)(2,1)S(1)}, u32[]{:S(2)}, u32[]{:S(2)}) collective-permute-start(bf16[128,128]{1,0:T(8,128)(2,1)S(1)} %record.1), channel_id=1, source_target_pairs={{0,32},{1,33},{2,34},{3,35},{4,36},{5,37},{6,38},{7,39},{8,12},{9,... | collective-permute-start | bytes 98312 | tf_op jit(solution)/shard_map/ppermute | solution.py:244
  7.0 0.8 %collective-permute-start.1 = (bf16[128,128]{1,0:T(8,128)(2,1)S(1)}, bf16[128,128]{1,0:T(8,128)(2,1)S(1)}, u32[]{:S(2)}, u32[]{:S(2)}) collective-permute-start(bf16[128,128]{1,0:T(8,128)(2,1)S(1)} %record.1), channel_id=1, source_target_pairs={{0,48},{1,49},{2,50},{3,51},{4,52},{5,53},{6,54},{7,55},{8,76},{9,... | collective-permute-start | bytes 98312 | tf_op jit(solution)/shard_map/ppermute | solution.py:244
  7.8 0.7 collective-permute-start
  8.5 1.3 %collective-permute-start.9 = (bf16[32,2048]{1,0:T(8,128)(2,1)S(1)}, bf16[32,2048]{1,0:T(8,128)(2,1)S(1)}, u32[]{:S(2)}, u32[]{:S(2)}) collective-permute-start(bf16[32,2048]{1,0:T(8,128)(2,1)S(1)} %copy-done), channel_id=1, source_target_pairs={{0,8},{1,9},{2,10},{3,11},{4,12},{5,13},{6,14},{7,15},{8,0},{9,1},... | collective-permute-start | bytes 393224 | tf_op jit(solution)/shard_map/ppermute | solution.py:241
  9.9 0.0 collective-permute-done.2
  9.9 0.0 collective-permute-done.1
  9.9 1.9 %collective-permute-done = bf16[128,128]{1,0:T(8,128)(2,1)S(1)} collective-permute-done((bf16[128,128]{1,0:T(8,128)(2,1)S(1)}, bf16[128,128]{1,0:T(8,128)(2,1)S(1)}, u32[]{:S(2)}, u32[]{:S(2)}) %collective-permute-start) | collective-permute-done | bytes 32800 | tf_op jit(solution)/shard_map/ppermute | solution.py:244
  11.8 3.7 %collective-permute-start.5 = (bf16[512,128]{1,0:T(8,128)(2,1)S(1)}, bf16[512,128]{1,0:T(8,128)(2,1)S(1)}, u32[]{:S(2)}, u32[]{:S(2)}) collective-permute-start(bf16[512,128]{1,0:T(8,128)(2,1)S(1)} %pad_maximum_fusion), channel_id=1, source_target_pairs={{0,4},{1,5},{2,6},{3,7},{4,0},{5,1},{6,2},{7,3},{8,10},{9,11},{10,... | collective-permute-start | bytes 393224 | tf_op jit(solution)/shard_map/ppermute | solution.py:244
  15.5 0.4 collective-permute-start.4
  15.9 1.0 %collective-permute-start.3 = (bf16[512,128]{1,0:T(8,128)(2,1)S(1)}, bf16[512,128]{1,0:T(8,128)(2,1)S(1)}, u32[]{:S(2)}, u32[]{:S(2)}) collective-permute-start(bf16[512,128]{1,0:T(8,128)(2,1)S(1)} %pad_maximum_fusion), channel_id=1, source_target_pairs={{0,64},{1,65},{2,66},{3,67},{4,68},{5,69},{6,70},{7,71},{8,9},{9,1... | collective-permute-start | bytes 393224 | tf_op jit(solution)/shard_map/ppermute | solution.py:244
  17.0 4.0 %collective-permute-done.3 = bf16[512,128]{1,0:T(8,128)(2,1)S(1)} collective-permute-done((bf16[512,128]{1,0:T(8,128)(2,1)S(1)}, bf16[512,128]{1,0:T(8,128)(2,1)S(1)}, u32[]{:S(2)}, u32[]{:S(2)}) %collective-permute-start.3) | collective-permute-done | bytes 131104 | tf_op jit(solution)/shard_map/ppermute | solution.py:244
  21.0 0.0 collective-permute-done.4
  21.0 0.0 collective-permute-done.5
  21.0 2.8 %collective-permute-start.7 = (bf16[2048,128]{1,0:T(8,128)(2,1)S(1)}, bf16[2048,128]{1,0:T(8,128)(2,1)S(1)}, u32[]{:S(2)}, u32[]{:S(2)}) collective-permute-start(bf16[2048,128]{1,0:T(8,128)(2,1)S(1)} %constant_dynamic-update-slice_fusion.refs_0_), channel_id=1, source_target_pairs={{0,3},{1,0},{2,1},{3,2},{4,7},{5,4},{6,5},{7,6},{8,56},{9,57},{10,... | collective-permute-start | bytes 1572872 | tf_op jit(solution)/shard_map/ppermute | solution.py:248
  23.9 0.0 collective-permute-start.6
  23.9 0.1 operand.2.refs_1_.refs_2_
  24.0 0.0 collective-permute-done.9.pixels_ref
  24.0 0.1 operand.3.refs_2_.refs_3_.refs_1_
  24.1 7.2 %accumulate.4 = (f32[80,2048]{1,0:T(8,128)S(1)}, f32[80,2048]{1,0:T(8,128)S(1)}) custom-call(bf16[2048,128]{1,0:T(8,128)(2,1)S(1)} %constant_dynamic-update-slice_fusion.refs_0_, bf16[128,2048]{1,0:T(8,128)(2,1)S(1)} %operand.2.refs_1_.refs_2_, bf16[128,2048]{1,0:T(8,128)(2,1)S(1)} %operand.3.refs_2_.refs_3_.refs_1_), custom_call_target="tpu_custom_call" | custom-call | flops 4294967296 | bytes 524288 | tf_op jit(solution)/shard_map/accumulate/pallas_call | solution.py:146
  31.3 0.0 collective-permute-done.7.refs_1_
  31.3 2.2 %collective-permute-done.6.refs_0_ = bf16[2048,128]{1,0:T(8,128)(2,1)S(1)} collective-permute-done((bf16[2048,128]{1,0:T(8,128)(2,1)S(1)}, bf16[2048,128]{1,0:T(8,128)(2,1)S(1)}, u32[]{:S(2)}, u32[]{:S(2)}) %collective-permute-start.6) | collective-permute-done | bytes 524320 | tf_op jit(solution)/shard_map/ppermute | solution.py:247
  33.4 0.0 collective-permute-start.8
  33.4 13.0 %accumulate.5 = (f32[80,2048]{1,0:T(8,128)S(1)}, f32[80,2048]{1,0:T(8,128)S(1)}) custom-call(bf16[2048,128]{1,0:T(8,128)(2,1)S(1)} %collective-permute-done.6.refs_0_, bf16[2048,128]{1,0:T(8,128)(2,1)S(1)} %collective-permute-done.7.refs_1_, bf16[128,2048]{1,0:T(8,128)(2,1)S(1)} %operand.2.refs_1_.refs_2_, ...), custom_call_target="tpu_custom_call", output_to_operand_aliasing={{0}: (4, {}), {1}: (5, {})} | custom-call | flops 8589934592 | bytes 1048576 | tf_op jit(solution)/shard_map/accumulate/pallas_call | solution.py:146
  46.4 0.0 collective-permute-done.8.refs_0_
  46.4 4.0 %accumulate.7 = f32[80,2048]{1,0:T(8,128)S(1)} custom-call(bf16[2048,128]{1,0:T(8,128)(2,1)S(1)} %collective-permute-done.8.refs_0_, bf16[128,2048]{1,0:T(8,128)(2,1)S(1)} %operand.3.refs_2_.refs_3_.refs_1_, f32[80,2048]{1,0:T(8,128)S(1)} %get-tuple-element.18.refs_2_), custom_call_target="tpu_custom_call", output_to_operand_aliasing={{}: (2, {})} | custom-call | flops 2147483648 | bytes 524288 | tf_op jit(solution)/shard_map/accumulate/pallas_call | solution.py:146
  50.4 5.9 %collective-permute-start.10 = (f32[80,2048]{1,0:T(8,128)S(1)}, f32[80,2048]{1,0:T(8,128)S(1)}, u32[]{:S(2)}, u32[]{:S(2)}) collective-permute-start(f32[80,2048]{1,0:T(8,128)S(1)} %accumulate.7), channel_id=1, source_target_pairs={{0,8},{1,9},{2,10},{3,11},{4,12},{5,13},{6,14},{7,15},{8,0},{9,1},... | collective-permute-start | bytes 1966088 | tf_op jit(solution)/shard_map/ppermute | solution.py:254
  56.3 4.0 %accumulate.6.mine_ref = f32[80,2048]{1,0:T(8,128)S(1)} custom-call(bf16[2048,128]{1,0:T(8,128)(2,1)S(1)} %collective-permute-done.8.refs_0_, bf16[128,2048]{1,0:T(8,128)(2,1)S(1)} %operand.2.refs_1_.refs_2_, f32[80,2048]{1,0:T(8,128)S(1)} %get-tuple-element.17.refs_2_), custom_call_target="tpu_custom_call", output_to_operand_aliasing={{}: (2, {})} | custom-call | flops 2147483648 | bytes 524288 | tf_op jit(solution)/shard_map/accumulate/pallas_call | solution.py:146
  60.3 0.0 collective-permute-done.10.theirs_ref
  60.3 0.2 scale.1
  60.6 13.7 %all_to_all.8 = f32[128,1,128]{2,1,0:T(1,128)S(1)} all-to-all(f32[128,1,128]{2,1,0:T(1,128)S(1)} %broadcast_in_dim.2), channel_id=1, replica_groups=mesh['ylo'=2,'x'=4,'core'=2,'yhi'=2,'z'=4] {'ylo','x','core','yhi','z'}, dimensions={0} | all-to-all | bytes 131072 | tf_op jit(solution)/shard_map/all_to_all | solution.py:217
  74.3 1.0 %finish.1 = (f32[64,2048]{1,0:T(8,128)}, f32[1,2048]{1,0:T(1,128)}) custom-call(f32[128,128]{1,0:T(8,128)S(1)} %bitcast.2, f32[64,2048]{1,0:T(8,128)S(1)} %get-tuple-element.20.scaled_ref, f32[1,2048]{1,0:T(1,128)S(1)} %get-tuple-element.21.degree_ref), custom_call_target="tpu_custom_call" | custom-call | tf_op jit(solution)/shard_map/finish/pallas_call | solution.py:202
  (9 shorter events, 0.1 us)
Async XLA Ops:
  0.6 0.7 copy-start.2
  1.3 0.9 %copy-start = (bf16[32,2048]{1,0:T(8,128)(2,1)S(1)}, bf16[32,2048]{1,0:T(8,128)(2,1)}, u32[]{:S(2)}) copy-start(bf16[32,2048]{1,0:T(8,128)(2,1)} %pixels_ref.3) | copy-start | bytes 393220
  2.2 0.7 copy-start.1
  3.2 6.6 %collective-permute-start.2 = (bf16[128,128]{1,0:T(8,128)(2,1)S(1)}, bf16[128,128]{1,0:T(8,128)(2,1)S(1)}, u32[]{:S(2)}, u32[]{:S(2)}) collective-permute-start(bf16[128,128]{1,0:T(8,128)(2,1)S(1)} %record.1), channel_id=1, source_target_pairs={{0,32},{1,33},{2,34},{3,35},{4,36},{5,37},{6,38},{7,39},{8,12},{9,... | collective-permute-start | bytes 98312 | tf_op jit(solution)/shard_map/ppermute | solution.py:244
  7.0 2.8 %collective-permute-start.1 = (bf16[128,128]{1,0:T(8,128)(2,1)S(1)}, bf16[128,128]{1,0:T(8,128)(2,1)S(1)}, u32[]{:S(2)}, u32[]{:S(2)}) collective-permute-start(bf16[128,128]{1,0:T(8,128)(2,1)S(1)} %record.1), channel_id=1, source_target_pairs={{0,48},{1,49},{2,50},{3,51},{4,52},{5,53},{6,54},{7,55},{8,76},{9,... | collective-permute-start | bytes 98312 | tf_op jit(solution)/shard_map/ppermute | solution.py:244
  7.8 4.0 %collective-permute-start = (bf16[128,128]{1,0:T(8,128)(2,1)S(1)}, bf16[128,128]{1,0:T(8,128)(2,1)S(1)}, u32[]{:S(2)}, u32[]{:S(2)}) collective-permute-start(bf16[128,128]{1,0:T(8,128)(2,1)S(1)} %record.1), channel_id=1, source_target_pairs={{0,16},{1,17},{2,18},{3,19},{4,20},{5,21},{6,22},{7,23},{8,72},{9,... | collective-permute-start | bytes 98312 | tf_op jit(solution)/shard_map/ppermute | solution.py:244
  8.5 15.5 %collective-permute-start.9 = (bf16[32,2048]{1,0:T(8,128)(2,1)S(1)}, bf16[32,2048]{1,0:T(8,128)(2,1)S(1)}, u32[]{:S(2)}, u32[]{:S(2)}) collective-permute-start(bf16[32,2048]{1,0:T(8,128)(2,1)S(1)} %copy-done), channel_id=1, source_target_pairs={{0,8},{1,9},{2,10},{3,11},{4,12},{5,13},{6,14},{7,15},{8,0},{9,1},... | collective-permute-start | bytes 393224 | tf_op jit(solution)/shard_map/ppermute | solution.py:241
  11.8 9.2 %collective-permute-start.5 = (bf16[512,128]{1,0:T(8,128)(2,1)S(1)}, bf16[512,128]{1,0:T(8,128)(2,1)S(1)}, u32[]{:S(2)}, u32[]{:S(2)}) collective-permute-start(bf16[512,128]{1,0:T(8,128)(2,1)S(1)} %pad_maximum_fusion), channel_id=1, source_target_pairs={{0,4},{1,5},{2,6},{3,7},{4,0},{5,1},{6,2},{7,3},{8,10},{9,11},{10,... | collective-permute-start | bytes 393224 | tf_op jit(solution)/shard_map/ppermute | solution.py:244
  15.5 5.5 %collective-permute-start.4 = (bf16[512,128]{1,0:T(8,128)(2,1)S(1)}, bf16[512,128]{1,0:T(8,128)(2,1)S(1)}, u32[]{:S(2)}, u32[]{:S(2)}) collective-permute-start(bf16[512,128]{1,0:T(8,128)(2,1)S(1)} %pad_maximum_fusion), channel_id=1, source_target_pairs={{0,68},{1,69},{2,70},{3,71},{4,64},{5,65},{6,66},{7,67},{8,11},{9,... | collective-permute-start | bytes 393224 | tf_op jit(solution)/shard_map/ppermute | solution.py:244
  15.9 5.0 %collective-permute-start.3 = (bf16[512,128]{1,0:T(8,128)(2,1)S(1)}, bf16[512,128]{1,0:T(8,128)(2,1)S(1)}, u32[]{:S(2)}, u32[]{:S(2)}) collective-permute-start(bf16[512,128]{1,0:T(8,128)(2,1)S(1)} %pad_maximum_fusion), channel_id=1, source_target_pairs={{0,64},{1,65},{2,66},{3,67},{4,68},{5,69},{6,70},{7,71},{8,9},{9,1... | collective-permute-start | bytes 393224 | tf_op jit(solution)/shard_map/ppermute | solution.py:244
  21.0 10.2 %collective-permute-start.7 = (bf16[2048,128]{1,0:T(8,128)(2,1)S(1)}, bf16[2048,128]{1,0:T(8,128)(2,1)S(1)}, u32[]{:S(2)}, u32[]{:S(2)}) collective-permute-start(bf16[2048,128]{1,0:T(8,128)(2,1)S(1)} %constant_dynamic-update-slice_fusion.refs_0_), channel_id=1, source_target_pairs={{0,3},{1,0},{2,1},{3,2},{4,7},{5,4},{6,5},{7,6},{8,56},{9,57},{10,... | collective-permute-start | bytes 1572872 | tf_op jit(solution)/shard_map/ppermute | solution.py:248
  23.9 9.5 %collective-permute-start.6 = (bf16[2048,128]{1,0:T(8,128)(2,1)S(1)}, bf16[2048,128]{1,0:T(8,128)(2,1)S(1)}, u32[]{:S(2)}, u32[]{:S(2)}) collective-permute-start(bf16[2048,128]{1,0:T(8,128)(2,1)S(1)} %constant_dynamic-update-slice_fusion.refs_0_), channel_id=1, source_target_pairs={{0,1},{1,2},{2,3},{3,0},{4,5},{5,6},{6,7},{7,4},{8,24},{9,25},{10,... | collective-permute-start | bytes 1572872 | tf_op jit(solution)/shard_map/ppermute | solution.py:247
  33.4 13.0 %collective-permute-start.8 = (bf16[2048,128]{1,0:T(8,128)(2,1)S(1)}, bf16[2048,128]{1,0:T(8,128)(2,1)S(1)}, u32[]{:S(2)}, u32[]{:S(2)}) collective-permute-start(bf16[2048,128]{1,0:T(8,128)(2,1)S(1)} %constant_dynamic-update-slice_fusion.refs_0_), channel_id=1, source_target_pairs={{0,2},{1,3},{2,0},{3,1},{4,6},{5,7},{6,4},{7,5},{8,40},{9,41},{10,... | collective-permute-start | bytes 1572872 | tf_op jit(solution)/shard_map/ppermute | solution.py:251
  50.4 9.9 %collective-permute-start.10 = (f32[80,2048]{1,0:T(8,128)S(1)}, f32[80,2048]{1,0:T(8,128)S(1)}, u32[]{:S(2)}, u32[]{:S(2)}) collective-permute-start(f32[80,2048]{1,0:T(8,128)S(1)} %accumulate.7), channel_id=1, source_target_pairs={{0,8},{1,9},{2,10},{3,11},{4,12},{5,13},{6,14},{7,15},{8,0},{9,1},... | collective-permute-start | bytes 1966088 | tf_op jit(solution)/shard_map/ppermute | solution.py:254
